TPU v7x, 32 devices: a whole 2x2x4 slice. The times are simulated.
32 devices in a mesh: grp: 2 (over y), samp: 4 (over z), snp: 4 (over x, core).
Axes of the slice: x: 2, y: 2, z: 4, core: 2. Of those that a mesh axis runs over, the one named last changes fastest.
Arguments:
- genotypes: int32 [2048, 8192], P(('grp', 'samp'), 'snp'), parts along dimension 0, may hold values from 0 to 2730, as said below
- basis_cols: bfloat16 [16384, 256], P(('grp', 'snp')), parts along dimension 0, may hold values from -0.0625 to 0.0625
Outputs:
- y_block: float32 [8, 4, 512, 256], P(('grp', 'snp'), 'samp'), parts along dimension 0
- r_factor: float32 [512, 256], P('grp'), parts along dimension 0
- q_next: float32 [8, 4, 512, 256], P(('grp', 'snp'), 'samp'), parts along dimension 0
There are 2 independent parts, one for each index of `grp`. A program takes and returns all parts, laid end to end along the dimension named above; each array names one. Nothing has to cross between parts.
Inputs may be any that keep to these rules, and one draw needn't show every extreme that they name: `genotypes`: each word packs 6 dosages of 0, 1 or 2 in pairs of bits: bits 2 t and 2 t + 1 of word (w, p) hold the dosage of sample 6 w + t at SNP p, t from 0 to 5; bits 12 and up are zero.
All inputs are finite; a program needn't handle non-finite values.
Results may differ from a plain program's by a relative error of at most 0.0025.
Values may be sent and summed in bfloat16 or wider, within the bound.
A program may use at most 64 MiB of HBM per device.

v0:
```python
import jax
import jax.numpy as jnp
from jax import lax
from jax.sharding import PartitionSpec as P


def unpack_counts(genotypes):
    planes = [
        jnp.bitwise_and(jnp.right_shift(genotypes, 2 * shift_pos), 3) for shift_pos in range(6)
    ]
    local_counts = planes[0].sum(axis=0)
    for plane_item in planes[1:]:
        local_counts = local_counts + plane_item.sum(axis=0)
    dosage = jnp.stack([plane_item.astype(jnp.bfloat16) for plane_item in planes], axis=1)
    dosage = dosage.reshape(genotypes.shape[0] * 6, genotypes.shape[1])
    return (dosage, local_counts)


def per_device(genotypes, basis_cols):
    dosage, local_counts = unpack_counts(genotypes)
    sample_rows, snp_cols = dosage.shape
    width = basis_cols.shape[1]
    totals = lax.psum(local_counts, "samp")
    samples = sample_rows * lax.axis_size("samp")
    allele_mean = totals.astype(jnp.float32) / jnp.float32(samples)
    center = jnp.dot(allele_mean, basis_cols.astype(jnp.float32), precision=lax.Precision.HIGHEST)
    inv_root = jnp.float32(1.0) / jnp.sqrt(jnp.float32(samples))
    contract_rows = (((0,), (0,)), ((), ()))
    product_term = jnp.dot(dosage, basis_cols, preferred_element_type=jnp.float32) - center[None, :]
    score_rows = lax.psum(product_term, "snp").astype(jnp.bfloat16)
    y_local = lax.psum_scatter(
        lax.dot_general(dosage, score_rows, contract_rows, preferred_element_type=jnp.float32)
        * inv_root,
        "samp",
        scatter_dimension=0,
        tiled=True,
    )
    snp_total = snp_cols * lax.axis_size("snp")
    local_gram = jnp.dot(y_local.T, y_local, precision=lax.Precision.HIGHEST) / jnp.float32(
        snp_total
    )
    gram_sum = lax.psum(local_gram, ("samp", "snp"))
    lower_factor = jnp.linalg.cholesky(gram_sum)
    q_next = lax.linalg.triangular_solve(
        lower_factor, y_local, left_side=False, lower=True, transpose_a=True
    )
    layout = (1, 1, y_local.shape[0], width)
    return (y_local.reshape(layout), lower_factor.T, q_next.reshape(layout))


def solution(mesh):
    return jax.shard_map(
        per_device,
        mesh=mesh,
        in_specs=(P(("grp", "samp"), "snp"), P(("grp", "snp"), None)),
        out_specs=(
            P(("grp", "snp"), "samp", None, None),
            P("grp", None),
            P(("grp", "snp"), "samp", None, None),
        ),
        check_vma=False,
    )
```

profile of v0, /device:TPU:0, one launch (start us, length us, event | category | flops | bytes accessed | tf_op | source)
XLA Modules:
  0.0 291.1 jit_solution(1570081549035918999)
XLA Ops:
  7.2 0.0 copy-start
  7.2 0.0 copy-start.1
  7.2 0.0 reduce-scatter.2.cloned.1.call-start
  7.2 2.0 fusion.23
  9.2 0.3 copy-done.1
  9.5 1.2 fusion.2
  10.7 0.3 fusion.21
  11.0 0.3 fusion.19
  11.3 0.3 fusion.17
  11.5 0.3 fusion.15
  11.8 0.3 fusion.13
  12.1 6.9 %copy.9 = bf16[256,6,2048]{2,1,0:T(8,128)(2,1)} copy(bf16[256,6,2048]{2,0,1:T(8,128)(2,1)S(1)} %fusion.13) | data formatting | bytes 12582912 | tf_op jit(solution)/shard_map/stack | solution.py:14
  18.9 11.1 %reshape.33 = bf16[1536,2048]{1,0:T(8,128)(2,1)} reshape(bf16[256,6,2048]{2,1,0:T(8,128)(2,1)} %copy.9) | data formatting | bytes 12582912 | tf_op jit(solution)/shard_map/reshape | solution.py:15
  30.0 10.0 %psum.21 = s32[2048]{0:T(1024)S(1)} all-reduce(s32[2048]{0:T(1024)S(1)} %add_add_fusion), channel_id=1, replica_groups=mesh['grp'=2,'samp'=4,'snp'=4] {'samp'}, use_global_device_ids=true, to_apply=%region_6.0 | all-reduce | flops 2048 | bytes 16384 | tf_op jit(solution)/shard_map/psum | solution.py:23
  40.1 0.0 copy-done
  40.1 0.5 fusion.36
  40.6 4.6 %convolution_subtract_fusion = f32[1536,256]{1,0:T(8,128)S(1)} fusion(bf16[1536,2048]{1,0:T(8,128)(2,1)} %reshape.33, bf16[2048,256]{1,0:T(8,128)(2,1)S(1)} %copy-done, f32[256]{0:T(256)S(1)} %bitcast.72), kind=kOutput, calls=%fused_computation.3 | convolution fusion | flops 1611005952 | bytes 8913920 | tf_op jit(solution)/shard_map/dot_general | solution.py:29
  45.2 32.6 %all-reduce.5 = bf16[1536,256]{1,0:T(8,128)(2,1)S(1)} all-reduce(f32[1536,256]{1,0:T(8,128)S(1)} %convolution_subtract_fusion), channel_id=1, replica_groups=mesh['grp'=2,'samp'=4,'snp'=4] {'snp'}, use_global_device_ids=true, to_apply=%region_7.0 | all-reduce | flops 393216 | bytes 2359296 | tf_op jit(solution)/shard_map/psum | solution.py:30
  77.8 6.0 %convolution_multiply_fusion = f32[2048,256]{1,0:T(8,128)} fusion(bf16[1536,2048]{1,0:T(8,128)(2,1)} %reshape.33, bf16[1536,256]{1,0:T(8,128)(2,1)S(1)} %all-reduce.5), kind=kOutput, calls=%fused_computation.2 | convolution fusion | flops 1611137024 | bytes 9175040 | tf_op jit(solution)/shard_map/dot_general | solution.py:32
  83.8 0.0 reduce-scatter.2.cloned.1.call-update
  83.9 0.0 all-reduce.4.cloned.1.call-start
  83.9 42.3 %reduce-scatter.2.cloned.1.call-done = f32[512,256]{1,0:T(8,128)} async-done(((f32[2048,256]{1,0:T(8,128)}), f32[512,256]{1,0:T(8,128)}) %reduce-scatter.2.cloned.1.call-update) | async-done | bytes 524304 | tf_op jit(solution)/shard_map/reduce_scatter | solution.py:31
  126.2 2.9 convolution_multiply_fusion.1
  129.1 0.0 all-reduce.4.cloned.1.call-update
  129.2 90.0 %all-reduce.4.cloned.1.call-done = f32[256,256]{0,1:T(8,128)} async-done(((f32[256,256]{0,1:T(8,128)}), f32[256,256]{0,1:T(8,128)}) %all-reduce.4.cloned.1.call-update) | async-done | bytes 262160 | tf_op jit(solution)/shard_map/psum | solution.py:42
  219.2 1.1 copy.11
  220.2 0.0 copy-start.2
  220.3 1.0 fusion.27
  221.3 11.7 %cholesky.50 = f32[128,128]{1,0:T(8,128)S(1)} custom-call(f32[128,128]{1,0:T(8,128)S(1)} %cholesky.118), custom_call_target="Cholesky" | custom-call | tf_op jit(solution)/shard_map/jit(cholesky)/cholesky | solution.py:43
  233.1 9.8 %custom-call.14 = f32[1,128,128]{1,2,0:T(8,128)S(1)} custom-call(f32[1,128,128]{2,1,0:T(8,128)S(1)} %get-tuple-element.38), custom_call_target="InvertDiagBlocksLowerTriangular" | custom-call | tf_op jit(solution)/shard_map/jit(cholesky)/cholesky | solution.py:43
  242.9 0.2 constant_dynamic-update-slice_fusion.1
  243.1 0.3 convolution_subtract_fusion.2
  243.4 11.7 %cholesky.105 = f32[128,128]{1,0:T(8,128)S(1)} custom-call(f32[128,128]{1,0:T(8,128)S(1)} %convolution_subtract_fusion.2), custom_call_target="Cholesky" | custom-call | tf_op jit(solution)/shard_map/jit(cholesky)/cholesky | solution.py:43
  255.1 0.6 compare_reduce_fusion
  257.1 0.8 copy.12
  258.0 0.1 triangular_solve.43
  258.0 4.1 %while.1 = (s32[]{:T(128)}, f32[256,256]{1,0:T(8,128)S(1)}, s32[2,2]{1,0:T(2,128)S(1)}, f32[2,128,128]{2,1,0:T(8,128)S(1)}, s32[]{:T(128)}) while((s32[]{:T(128)}, f32[256,256]{1,0:T(8,128)S(1)}, s32[2,2]{1,0:T(2,128)S(1)}, f32[2,128,128]{2,1,0:T(8,128)S(1)}, s32[]{:T(128)}) %tuple.35), condition=%wide.while_cond, body=%wide.while_body.sunk | while | flops 2 | bytes 131189 | solution.py:44
  258.0 0.6 fusion.50
  258.6 1.4 bitcast_dynamic-update-slice_fusion.2
  260.1 0.6 fusion.50
  260.7 1.4 bitcast_dynamic-update-slice_fusion.2
  262.1 19.7 %custom-call.15 = f32[2,128,128]{1,2,0:T(8,128)S(1)} custom-call(f32[2,128,128]{2,1,0:T(8,128)S(1)} %get-tuple-element.10), custom_call_target="InvertDiagBlocksLowerTriangular" | custom-call | tf_op jit(solution)/shard_map/triangular_solve | solution.py:44
  281.8 0.0 copy-done.2
  281.8 0.4 fusion.25
  282.2 0.6 convolution_subtract_fusion.1
  282.8 0.4 fusion.30
  283.3 1.0 copy.13
  (12 shorter events, 0.2 us)
Async XLA Ops:
  7.2 32.9 %copy-start = (bf16[2048,256]{1,0:T(8,128)(2,1)S(1)}, bf16[2048,256]{1,0:T(8,128)(2,1)}, u32[]{:S(2)}) copy-start(bf16[2048,256]{1,0:T(8,128)(2,1)} %param.3) | copy-start | bytes 3145732
  7.2 2.3 copy-start.1
  7.2 119.0 %reduce-scatter.2.cloned.1.call-start = ((), (), s32[]{:S(2)}) async-start(), calls=%async_computation.1 | async-start | bytes 2621440 | tf_op jit(solution)/shard_map/reduce_scatter | solution.py:31
  83.9 135.3 %all-reduce.4.cloned.1.call-start = ((), (), s32[]{:S(2)}) async-start(), calls=%async_computation.2 | async-start | bytes 524288 | tf_op jit(solution)/shard_map/psum | solution.py:42
  220.2 61.6 %copy-start.2 = (f32[512,256]{1,0:T(8,128)S(1)}, f32[512,256]{1,0:T(8,128)}, u32[]{:S(2)}) copy-start(f32[512,256]{1,0:T(8,128)} %reduce-scatter.2.cloned.1.call-done) | copy-start | bytes 1572868
Sparse Core Ops, SparseCore 0:
  84.0 42.1 reduce-scatter.1
  130.2 88.9 all-reduce.3
where the time goes:
time: 292 us; the launch traced here: 291 us
  waiting for transfers between devices  132 us (45%)
  other arithmetic  59.3 us (20%)
  blocking collectives  42.7 us (15%)
  local copies, waits for them, and re-layouts  25.3 us (9%)
  matrix products  15.9 us (5%)
  between operations  15.6 us (5%)
    psum x1, waiting for transfers between devices, per_device(): gram_sum = lax.psum(local_gram, ('samp', 'snp'))  90 us
    reduce_scatter x1, waiting for transfers between devices, per_device(): lax.psum_scatter(lax.dot_general(dosage, score_rows, contract_rows, prefe...  42.3 us
    another operation x6, other arithmetic, per_device(): lower_factor = jnp.linalg.cholesky(gram_sum)  33.9 us
    psum x1, blocking collectives, per_device(): score_rows = lax.psum(product_term, 'snp').astype(jnp.bfloat16)  32.6 us
    another operation x3, other arithmetic, per_device(): lax.linalg.triangular_solve(lower_factor, y_local, left_side=False, lower...  19.7 us
    reshape x1, local copies, waits for them, and re-layouts, unpack_counts(): dosage = dosage.reshape(genotypes.shape[0] * 6, genotypes.shape[1])  11.1 us
    psum x1, blocking collectives, per_device(): totals = lax.psum(local_counts, 'samp')  10 us
    another operation x1, local copies, waits for them, and re-layouts, unpack_counts(): jnp.stack([plane_item.astype(jnp.bfloat16) for plane_item in planes], axi...  6.86 us
  transfers between devices with their start and end apart: 2, of which 2 were waited for; matrix products, arithmetic and copies ran while one was open for 0% of the time, Pallas kernels for 0%

commit v1 on v0

--- a/solution.py
+++ b/solution.py
@@ -39,7 +39,7 @@
     local_gram = jnp.dot(y_local.T, y_local, precision=lax.Precision.HIGHEST) / jnp.float32(
         snp_total
     )
-    gram_sum = lax.psum(local_gram, ("samp", "snp"))
+    gram_sum = lax.all_gather(local_gram, ("samp", "snp")).sum(axis=0)
     lower_factor = jnp.linalg.cholesky(gram_sum)
     q_next = lax.linalg.triangular_solve(
         lower_factor, y_local, left_side=False, lower=True, transpose_a=True

time: 292 us -> 252 us (0.86)
  waiting for transfers between devices: 132 us -> 92 us
    psum x1 -> x0, waiting for transfers between devices: 90 us -> none  [per_device(): gram_sum = lax.psum(local_gram, ('samp', 'snp'))]
    all_gather x0 -> x1, waiting for transfers between devices: none -> 49.7 us  [per_device(): gram_sum = lax.all_gather(local_gram, ('samp', 'snp')).sum(axis=0)]
where the time goes in v1:
time: 252 us; the launch traced here: 251 us
  waiting for transfers between devices  92 us (37%)
  other arithmetic  60.8 us (24%)
  blocking collectives  42.7 us (17%)
  local copies, waits for them, and re-layouts  24.3 us (10%)
  matrix products  16 us (6%)
  between operations  15.6 us (6%)
    all_gather x1, waiting for transfers between devices, per_device(): gram_sum = lax.all_gather(local_gram, ('samp', 'snp')).sum(axis=0)  49.7 us
    reduce_scatter x1, waiting for transfers between devices, per_device(): lax.psum_scatter(lax.dot_general(dosage, score_rows, contract_rows, prefe...  42.3 us
    another operation x6, other arithmetic, per_device(): lower_factor = jnp.linalg.cholesky(gram_sum)  33.9 us
    psum x1, blocking collectives, per_device(): score_rows = lax.psum(product_term, 'snp').astype(jnp.bfloat16)  32.6 us
    another operation x3, other arithmetic, per_device(): lax.linalg.triangular_solve(lower_factor, y_local, left_side=False, lower...  19.7 us
    reshape x1, local copies, waits for them, and re-layouts, unpack_counts(): dosage = dosage.reshape(genotypes.shape[0] * 6, genotypes.shape[1])  11.1 us
    psum x1, blocking collectives, per_device(): totals = lax.psum(local_counts, 'samp')  10 us
    another operation x1, local copies, waits for them, and re-layouts, unpack_counts(): jnp.stack([plane_item.astype(jnp.bfloat16) for plane_item in planes], axi...  6.86 us
  transfers between devices with their start and end apart: 2, of which 2 were waited for; matrix products, arithmetic and copies ran while one was open for 0% of the time, Pallas kernels for 0%

profile of v1, /device:TPU:0, one launch (start us, length us, event | category | flops | bytes accessed | tf_op | source)
XLA Modules:
  0.0 251.4 jit_solution(15746400675109472889)
XLA Ops:
  7.2 0.0 copy-start
  7.2 0.0 copy-start.1
  7.2 0.0 reduce-scatter.2.cloned.1.call-start
  7.2 2.0 fusion.23
  9.2 0.3 copy-done.1
  9.5 1.2 fusion.2
  10.7 0.3 fusion.21
  11.0 0.3 fusion.19
  11.3 0.3 fusion.17
  11.5 0.3 fusion.15
  11.8 0.3 fusion.13
  12.1 6.9 %copy.12 = bf16[256,6,2048]{2,1,0:T(8,128)(2,1)} copy(bf16[256,6,2048]{2,0,1:T(8,128)(2,1)S(1)} %fusion.13) | data formatting | bytes 12582912 | tf_op jit(solution)/shard_map/stack | solution.py:14
  18.9 11.1 %reshape.33 = bf16[1536,2048]{1,0:T(8,128)(2,1)} reshape(bf16[256,6,2048]{2,1,0:T(8,128)(2,1)} %copy.12) | data formatting | bytes 12582912 | tf_op jit(solution)/shard_map/reshape | solution.py:15
  30.0 10.0 %psum.14 = s32[2048]{0:T(1024)S(1)} all-reduce(s32[2048]{0:T(1024)S(1)} %add_add_fusion), channel_id=1, replica_groups=mesh['grp'=2,'samp'=4,'snp'=4] {'samp'}, use_global_device_ids=true, to_apply=%region_6.0 | all-reduce | flops 2048 | bytes 16384 | tf_op jit(solution)/shard_map/psum | solution.py:23
  40.1 0.0 copy-done
  40.1 0.5 fusion.36
  40.6 4.6 %convolution_subtract_fusion = f32[1536,256]{1,0:T(8,128)S(1)} fusion(bf16[1536,2048]{1,0:T(8,128)(2,1)} %reshape.33, bf16[2048,256]{1,0:T(8,128)(2,1)S(1)} %copy-done, f32[256]{0:T(256)S(1)} %bitcast.74), kind=kOutput, calls=%fused_computation.3 | convolution fusion | flops 1611005952 | bytes 8913920 | tf_op jit(solution)/shard_map/dot_general | solution.py:29
  45.2 32.6 %all-reduce.2 = bf16[1536,256]{1,0:T(8,128)(2,1)S(1)} all-reduce(f32[1536,256]{1,0:T(8,128)S(1)} %convolution_subtract_fusion), channel_id=1, replica_groups=mesh['grp'=2,'samp'=4,'snp'=4] {'snp'}, use_global_device_ids=true, to_apply=%region_7.0 | all-reduce | flops 393216 | bytes 2359296 | tf_op jit(solution)/shard_map/psum | solution.py:30
  77.8 6.0 %convolution_multiply_fusion = f32[2048,256]{1,0:T(8,128)} fusion(bf16[1536,2048]{1,0:T(8,128)(2,1)} %reshape.33, bf16[1536,256]{1,0:T(8,128)(2,1)S(1)} %all-reduce.2), kind=kOutput, calls=%fused_computation.2 | convolution fusion | flops 1611137024 | bytes 9175040 | tf_op jit(solution)/shard_map/dot_general | solution.py:32
  83.8 0.0 reduce-scatter.2.cloned.1.call-update
  83.9 0.0 all-gather.3.cloned.1.call-start
  83.9 42.3 %reduce-scatter.2.cloned.1.call-done = f32[512,256]{1,0:T(8,128)} async-done(((f32[2048,256]{1,0:T(8,128)}), f32[512,256]{1,0:T(8,128)}) %reduce-scatter.2.cloned.1.call-update) | async-done | bytes 524304 | tf_op jit(solution)/shard_map/reduce_scatter | solution.py:31
  126.2 2.9 %convolution_multiply_fusion.1 = f32[256,256]{1,0:T(8,128)} fusion(f32[512,256]{1,0:T(8,128)} %reduce-scatter.2.cloned.1.call-done), kind=kOutput, calls=%fused_computation.23 | convolution fusion | flops 402718720 | bytes 786432 | tf_op jit(solution)/shard_map/dot_general | solution.py:39
  129.1 0.0 all-gather.3.cloned.1.call-update
  129.2 49.7 %all-gather.3.cloned.1.call-done = f32[4096,256]{1,0:T(8,128)} async-done(((f32[256,256]{1,0:T(8,128)}), f32[4096,256]{1,0:T(8,128)}) %all-gather.3.cloned.1.call-update) | async-done | bytes 4194320 | tf_op jit(solution)/shard_map/all_gather | solution.py:42
  178.9 2.5 reduce_sum.69
  181.4 0.1 copy.13
  181.5 0.0 copy-start.2
  181.6 11.7 %cholesky.50 = f32[128,128]{1,0:T(8,128)S(1)} custom-call(f32[128,128]{1,0:T(8,128)S(1)} %cholesky.118), custom_call_target="Cholesky" | custom-call | tf_op jit(solution)/shard_map/jit(cholesky)/cholesky | solution.py:43
  193.3 9.8 %custom-call.14 = f32[1,128,128]{1,2,0:T(8,128)S(1)} custom-call(f32[1,128,128]{2,1,0:T(8,128)S(1)} %get-tuple-element.41), custom_call_target="InvertDiagBlocksLowerTriangular" | custom-call | tf_op jit(solution)/shard_map/jit(cholesky)/cholesky | solution.py:43
  203.1 0.2 constant_dynamic-update-slice_fusion.1
  203.4 0.3 convolution_subtract_fusion.2
  203.6 11.7 %cholesky.105 = f32[128,128]{1,0:T(8,128)S(1)} custom-call(f32[128,128]{1,0:T(8,128)S(1)} %convolution_subtract_fusion.2), custom_call_target="Cholesky" | custom-call | tf_op jit(solution)/shard_map/jit(cholesky)/cholesky | solution.py:43
  215.4 0.6 compare_reduce_fusion
  217.4 0.8 copy.14
  218.2 0.1 triangular_solve.43
  218.3 4.1 %while.1 = (s32[]{:T(128)}, f32[256,256]{1,0:T(8,128)S(1)}, s32[2,2]{1,0:T(2,128)S(1)}, f32[2,128,128]{2,1,0:T(8,128)S(1)}, s32[]{:T(128)}) while((s32[]{:T(128)}, f32[256,256]{1,0:T(8,128)S(1)}, s32[2,2]{1,0:T(2,128)S(1)}, f32[2,128,128]{2,1,0:T(8,128)S(1)}, s32[]{:T(128)}) %tuple.36), condition=%wide.while_cond, body=%wide.while_body.sunk | while | flops 2 | bytes 131189 | solution.py:44
  218.3 0.6 fusion.50
  218.9 1.4 bitcast_dynamic-update-slice_fusion.2
  220.3 0.6 fusion.50
  220.9 1.4 bitcast_dynamic-update-slice_fusion.2
  222.4 19.7 %custom-call.15 = f32[2,128,128]{1,2,0:T(8,128)S(1)} custom-call(f32[2,128,128]{2,1,0:T(8,128)S(1)} %get-tuple-element.10), custom_call_target="InvertDiagBlocksLowerTriangular" | custom-call | tf_op jit(solution)/shard_map/triangular_solve | solution.py:44
  242.1 0.0 copy-done.2
  242.1 0.4 fusion.25
  242.5 0.6 convolution_subtract_fusion.1
  243.1 0.4 fusion.30
  243.6 1.0 copy.15
  (13 shorter events, 0.2 us)
Async XLA Ops:
  7.2 32.9 %copy-start = (bf16[2048,256]{1,0:T(8,128)(2,1)S(1)}, bf16[2048,256]{1,0:T(8,128)(2,1)}, u32[]{:S(2)}) copy-start(bf16[2048,256]{1,0:T(8,128)(2,1)} %param.3) | copy-start | bytes 3145732
  7.2 2.3 copy-start.1
  7.2 119.0 %reduce-scatter.2.cloned.1.call-start = ((), (), s32[]{:S(2)}) async-start(), calls=%async_computation.1 | async-start | bytes 2621440 | tf_op jit(solution)/shard_map/reduce_scatter | solution.py:31
  83.9 95.0 %all-gather.3.cloned.1.call-start = ((), (), s32[]{:S(2)}) async-start(), calls=%async_computation.2 | async-start | bytes 4456448 | tf_op jit(solution)/shard_map/all_gather | solution.py:42
  181.5 60.6 %copy-start.2 = (f32[512,256]{1,0:T(8,128)S(1)}, f32[512,256]{1,0:T(8,128)}, u32[]{:S(2)}) copy-start(f32[512,256]{1,0:T(8,128)} %reduce-scatter.2.cloned.1.call-done) | copy-start | bytes 1572868
Sparse Core Ops, SparseCore 0:
  84.0 42.1 reduce-scatter.1
  129.3 49.5 all-gather.2
